TPU v7x, 256 devices: a whole 4x4x8 slice. The times are simulated.
256 devices in a mesh: col: 64 (over y, z, core), row: 4 (over x).
Axes of the slice: x: 4, y: 4, z: 8, core: 2. Of those that a mesh axis runs over, the one named last changes fastest.
Arguments:
- tile_left: bfloat16 [64, 8, 1024, 64], P('col', 'row'), may hold values from -0.41992188 to 0.41992188
- tile_right: bfloat16 [64, 8, 1024, 64], P('col', 'row'), may hold values from -0.1875 to 0.1875
- row_left: bfloat16 [64, 1024, 64], P('col'), may hold values from -0.41992188 to 0.41992188
- row_right: bfloat16 [64, 1024, 64], P('col'), may hold values from -0.1875 to 0.1875
- sketch: bfloat16 [1024, 64], replicated, may hold values from -6 to 6
- panel_left: bfloat16 [8, 1024, 64], P('row'), may hold values from -0.375 to 0.375
- panel_right: bfloat16 [8, 1024, 64], P('row'), may hold values from -0.1875 to 0.1875
- pivot_inverse: bfloat16 [1024, 1024], replicated, as said below
- band_inverse: bfloat16 [8, 1024, 1024], P('row'), as said below
- link_left: bfloat16 [8, 1024, 64], P('row'), may hold values from -0.75 to 0.75
- link_right: bfloat16 [8, 1024, 64], P('row'), may hold values from -0.0625 to 0.0625
- pivot_rhs: bfloat16 [1024, 32768], P(None, 'col'), may hold values from -6 to 6
- band_rhs: bfloat16 [8, 1024, 32768], P('row', None, 'col'), may hold values from -6 to 6
- carry_in: float32 [64, 32768], P(None, 'col'), may hold values from -3 to 3
Outputs:
- pivot_solution: bfloat16 [1024, 32768], P(None, 'col')
- schur_right: float32 [8, 1024, 64], P('row', 'col')
- band_solution: bfloat16 [8, 1024, 32768], P('row', None, 'col')
- link_states: float32 [8, 64, 32768], P('row', None, 'col')
Inputs may be any that keep to these rules, and one draw needn't show every extreme that they name: `pivot_inverse`: each tile is lower triangular with a positive diagonal, the inverse of a Cholesky factor of a diagonal covariance tile. `band_inverse`: each tile is lower triangular with a positive diagonal, the inverse of a Cholesky factor of a diagonal covariance tile.
All inputs are finite; a program needn't handle non-finite values.
Results may differ from a plain program's by a relative error of at most 0.0056.
Values sent between devices are 32-bit elements; how exact they have to be, the bound alone decides.
A program may use at most 128 MiB of HBM per device.

v0:
```python
import jax
import jax.numpy as jnp
from jax import lax
from jax.sharding import PartitionSpec as P

HIGHEST_PRECISION = lax.Precision.HIGHEST


def from_behind(block, axis, distance):
    devices = range(lax.axis_size(axis))
    route = [(i - distance, i) for i in devices if i - distance in devices]
    return lax.ppermute(block, axis, route)


def widened(array):
    return array.astype(jnp.float32)


def lower_inverse(gram_matrix):
    gram_lower = jnp.linalg.cholesky(gram_matrix)
    identity_matrix = jnp.broadcast_to(
        jnp.eye(gram_matrix.shape[-1], dtype=jnp.float32), gram_matrix.shape
    )
    return lax.linalg.triangular_solve(gram_lower, identity_matrix, left_side=True, lower=True)


def shards(
    tile_left,
    tile_right,
    row_left,
    row_right,
    sketch,
    panel_left,
    panel_right,
    pivot_inverse,
    band_inverse,
    link_left,
    link_right,
    pivot_rhs,
    band_rhs,
    carry_in,
):
    pivot_solution = jnp.dot(pivot_inverse, pivot_rhs, preferred_element_type=jnp.float32).astype(
        jnp.bfloat16
    )
    pulled = jnp.einsum(
        "nm,nc->mc", pivot_inverse, pivot_solution, preferred_element_type=jnp.float32
    )
    coupling = jnp.einsum(
        "jbnr,jns->jbrs", tile_right, row_right, preferred_element_type=jnp.float32
    )
    probe_core = jnp.einsum("jnr,ns->jrs", row_left, sketch, preferred_element_type=jnp.float32)
    sketch_core = jnp.einsum("jbrs,jst->jbrt", coupling, probe_core, precision=HIGHEST_PRECISION)
    left_wide = widened(tile_left)
    sketch_terms = jnp.einsum("jbnr,jbrt->bnt", left_wide, sketch_core, precision=HIGHEST_PRECISION)
    sketched = lax.psum(sketch_terms, "col")
    gram_matrix = jnp.einsum("bnr,bns->brs", sketched, sketched, precision=HIGHEST_PRECISION)
    inverse_low = lower_inverse(gram_matrix)
    panel_basis = jnp.einsum("bnr,bsr->bns", sketched, inverse_low, precision=HIGHEST_PRECISION)
    projected = jnp.einsum("jbnr,bns->jbrs", left_wide, panel_basis, precision=HIGHEST_PRECISION)
    middle = jnp.einsum("jbrs,jbrt->jbst", coupling, projected, precision=HIGHEST_PRECISION)
    schur_terms = jnp.einsum(
        "jns,jbst->bnt", widened(row_left), middle, precision=HIGHEST_PRECISION
    )
    schur_full = lax.psum(schur_terms, "col")
    slab_rows = schur_full.shape[1] // lax.axis_size("col")
    schur_right = lax.dynamic_slice_in_dim(
        schur_full, lax.axis_index("col") * slab_rows, slab_rows, 1
    )
    panel_coeffs = jnp.einsum(
        "bnr,nc->brc", widened(panel_right), pulled, precision=HIGHEST_PRECISION
    )
    schur_coeffs = jnp.einsum("bnr,nc->brc", schur_full, pulled, precision=HIGHEST_PRECISION)
    panel_term = jnp.einsum(
        "bnr,brc->bnc", widened(panel_left), panel_coeffs, precision=HIGHEST_PRECISION
    ) - jnp.einsum("bnr,brc->bnc", panel_basis, schur_coeffs, precision=HIGHEST_PRECISION)
    reduced = (band_rhs.astype(jnp.float32) - panel_term).astype(jnp.bfloat16)
    local_part = jnp.einsum(
        "bnm,bmc->bnc", band_inverse, reduced, preferred_element_type=jnp.float32
    )
    feed_columns = jnp.einsum(
        "bnm,bmr->bnr", band_inverse, link_left, preferred_element_type=jnp.float32
    )
    right_wide = widened(link_right)
    band_count = band_rhs.shape[0]
    leading = lax.axis_index("row") == 0

    def last_state(prior_state):
        for position in range(band_count):
            solved = local_part[position] - jnp.dot(
                feed_columns[position], prior_state, precision=HIGHEST_PRECISION
            )
            prior_state = jnp.einsum(
                "nr,nc->rc", right_wide[position], solved, precision=HIGHEST_PRECISION
            )
        return prior_state

    def relay_section(section_index, incoming_state):
        shifted = from_behind(last_state(incoming_state), "row", 1)
        return jnp.where(leading, carry_in, shifted)

    incoming = lax.fori_loop(0, lax.axis_size("row") - 1, relay_section, carry_in)
    solved_rows = []
    state_rows = []
    prior_state = incoming
    for position in range(band_count):
        solved = local_part[position] - jnp.dot(
            feed_columns[position], prior_state, precision=HIGHEST_PRECISION
        )
        prior_state = jnp.einsum(
            "nr,nc->rc", right_wide[position], solved, precision=HIGHEST_PRECISION
        )
        solved_rows.append(solved.astype(jnp.bfloat16))
        state_rows.append(prior_state)
    return (pivot_solution, schur_right, jnp.stack(solved_rows), jnp.stack(state_rows))


def solution(mesh):
    return jax.shard_map(
        shards,
        mesh=mesh,
        in_specs=(
            P("col", "row", None, None),
            P("col", "row", None, None),
            P("col", None, None),
            P("col", None, None),
            P(),
            P("row", None, None),
            P("row", None, None),
            P(),
            P("row", None, None),
            P("row", None, None),
            P("row", None, None),
            P(None, "col"),
            P("row", None, "col"),
            P(None, "col"),
        ),
        out_specs=(
            P(None, "col"),
            P("row", "col", None),
            P("row", None, "col"),
            P("row", None, "col"),
        ),
        check_vma=False,
    )
```

profile of v0, /device:TPU:2, one launch (start us, length us, event | category | flops | bytes accessed | tf_op | source)
XLA Modules:
  0.0 514.8 jit_solution(8060935407227560381)
XLA Ops:
  7.2 1.3 convolution_bitcast_fusion.5
  8.5 1.2 fusion.27
  10.1 2.1 convolution_bitcast_fusion.2
  15.0 4.4 fusion.48
  19.5 2.5 copy.31
  21.9 2.5 convolution_convert_fusion
  25.4 2.6 fusion.46
  28.0 170.8 %all-reduce.3.cloned.1.call-done = f32[2,1024,64]{1,2,0:T(8,128)} async-done(((f32[2,1024,64]{1,2,0:T(8,128)}), f32[2,1024,64]{1,2,0:T(8,128)}) %all-reduce.3.cloned.1.call-update) | async-done | bytes 524304 | tf_op jit(solution)/shard_map/psum | solution.py:56
  198.8 1.8 fusion.43
  201.3 1.5 fusion.39
  202.8 12.5 %custom-call.7 = f32[2,64,64]{2,1,0:T(8,128)S(1)} custom-call(f32[2,64,64]{2,1,0:T(8,128)} %fusion.39), custom_call_target="Cholesky" | custom-call | tf_op jit(solution)/shard_map/jit(cholesky)/cholesky | solution.py:20
  216.1 10.7 %custom-call.8 = f32[2,1,64,64]{2,3,1,0:T(8,128)S(1)} custom-call(f32[2,1,64,64]{3,2,1,0:T(8,128)} %select_bitcast_fusion), custom_call_target="InvertDiagBlocksLowerTriangular" | custom-call | tf_op jit(solution)/shard_map/triangular_solve | solution.py:24
  228.0 1.6 fusion.44
  230.4 1.3 convolution_bitcast_fusion.4
  233.1 3.6 fusion.22
  236.7 2.0 copy.36
  238.7 175.0 %all-reduce.5.cloned.1.call-done = f32[2,1024,64]{1,2,0:T(8,128)} async-done(((f32[2,1024,64]{1,2,0:T(8,128)}), f32[2,1024,64]{1,2,0:T(8,128)}) %all-reduce.5.cloned.1.call-update) | async-done | bytes 524304 | tf_op jit(solution)/shard_map/psum | solution.py:65
  413.7 4.0 fusion.20
  417.8 3.5 fusion.47
  421.3 2.3 fusion.17
  423.6 5.1 convolution_bitcast_fusion
  428.7 5.4 %copy.30 = f32[2,1024,512]{2,1,0:T(8,128)} copy(f32[2,1024,512]{1,2,0:T(8,128)} %convolution_bitcast_fusion) | data formatting | bytes 8388608 | tf_op jit(solution)/shard_map/while | solution.py:102
  434.1 55.4 %while.10 = (s32[]{:T(128)}, f32[64,512]{1,0:T(8,128)S(1)}, pred[]{:T(512)}, f32[2,1024,512]{2,1,0:T(8,128)}, f32[2,1024,64]{2,1,0:T(8,128)}, /*index=5*/f32[2,1...) while((s32[]{:T(128)}, f32[64,512]{1,0:T(8,128)S(1)}, pred[]{:T(512)}, f32[2,1024,512]{2,1,0:T(8,128)}, ...), condition=%wide.region_5.6_spmd, body=%wide.region_4.5_spmd.sunk | while | flops 1611694080 | bytes 35127476 | solution.py:102
  434.1 2.9 fusion.96
  437.1 5.2 %fusion.97 = f32[512,64]{1,0:T(8,128)S(1)} fusion(f32[1024,512]{1,0:T(8,128)S(1)} %fusion.96, f32[2,1024,512]{2,1,0:T(8,128)} %get-tuple-element.142, f32[2,1024,64]{2,1,0:T(8,128)S(1)} %get-tuple-element.144), kind=kOutput, calls=%fused_computation.3.clone.1 | convolution fusion | flops 403177472 | bytes 4849664 | tf_op jit(solution)/shard_map/while/body/eval_jaxpr/nr,nc->rc/dot_general | solution.py:93
  442.3 1.8 fusion.98
  444.1 1.5 fusion.99
  445.6 3.4 collective-permute-start
  449.0 3.5 collective-permute-done
  452.5 2.9 fusion.96
  455.5 5.2 %fusion.97 = f32[512,64]{1,0:T(8,128)S(1)} fusion(f32[1024,512]{1,0:T(8,128)S(1)} %fusion.96, f32[2,1024,512]{2,1,0:T(8,128)} %get-tuple-element.142, f32[2,1024,64]{2,1,0:T(8,128)S(1)} %get-tuple-element.144), kind=kOutput, calls=%fused_computation.3.clone.1 | convolution fusion | flops 403177472 | bytes 4849664 | tf_op jit(solution)/shard_map/while/body/eval_jaxpr/nr,nc->rc/dot_general | solution.py:93
  460.7 1.8 fusion.98
  462.5 1.5 fusion.99
  464.0 3.4 collective-permute-start
  467.4 3.5 collective-permute-done
  470.9 2.9 fusion.96
  473.9 5.2 %fusion.97 = f32[512,64]{1,0:T(8,128)S(1)} fusion(f32[1024,512]{1,0:T(8,128)S(1)} %fusion.96, f32[2,1024,512]{2,1,0:T(8,128)} %get-tuple-element.142, f32[2,1024,64]{2,1,0:T(8,128)S(1)} %get-tuple-element.144), kind=kOutput, calls=%fused_computation.3.clone.1 | convolution fusion | flops 403177472 | bytes 4849664 | tf_op jit(solution)/shard_map/while/body/eval_jaxpr/nr,nc->rc/dot_general | solution.py:93
  479.1 1.8 fusion.98
  480.9 1.5 fusion.99
  482.4 3.4 collective-permute-start
  485.8 3.5 collective-permute-done
  489.6 3.7 fusion.19
  493.3 1.2 fusion.30
  494.6 1.9 fusion.18
  496.4 1.3 convert_bitcast_fusion
  497.7 1.2 convolution_bitcast_fusion.3
  500.6 2.7 pad_maximum_fusion
  503.3 3.9 copy.35
  (64 shorter events, 11.4 us)
Async XLA Ops:
  7.2 14.7 %copy-start = (bf16[1024,1024]{1,0:T(8,128)(2,1)S(1)}, bf16[1024,1024]{1,0:T(8,128)(2,1)}, u32[]{:S(2)}) copy-start(bf16[1024,1024]{1,0:T(8,128)(2,1)} %param.23) | copy-start | bytes 6291460
  7.2 5.7 %copy-start.7 = (f32[64,512]{1,0:T(8,128)S(1)}, f32[64,512]{1,0:T(8,128)}, u32[]{:S(2)}) copy-start(f32[64,512]{1,0:T(8,128)} %param.29) | copy-start | bytes 393220
  7.2 5.7 %copy-start.12 = (bf16[2,1024,64]{1,2,0:T(8,128)(2,1)S(1)}, bf16[2,1024,64]{1,2,0:T(8,128)(2,1)}, u32[]{:S(2)}) copy-start(bf16[2,1024,64]{1,2,0:T(8,128)(2,1)} %param.26) | copy-start | bytes 786436
  7.2 191.6 %all-reduce.3.cloned.1.call-start = ((), (), s32[]{:S(2)}) async-start(), calls=%async_computation | async-start | bytes 1048576 | tf_op jit(solution)/shard_map/psum | solution.py:56
  12.2 401.5 %all-reduce.5.cloned.1.call-start = ((), (), s32[]{:S(2)}) async-start(), calls=%async_computation.1 | async-start | bytes 1048576 | tf_op jit(solution)/shard_map/psum | solution.py:65
  24.4 1.0 copy-start.11
  226.9 5.1 copy-start.14
  229.6 0.8 copy-start.5
  413.7 4.1 copy-start.6
  417.7 3.6 copy-start.9
  417.8 3.6 copy-start.10
  417.8 3.6 copy-start.15
  421.3 2.3 copy-start.8
  434.1 8.2 %copy-start.2 = (f32[2,1024,64]{2,1,0:T(8,128)S(1)}, f32[2,1024,64]{2,1,0:T(8,128)}, u32[]{:S(2)}) copy-start(f32[2,1024,64]{2,1,0:T(8,128)} %get-tuple-element.143) | copy-start | bytes 1572868 | tf_op jit(solution)/shard_map/while
  437.1 7.1 %copy-start.1 = (f32[2,1024,512]{2,1,0:T(8,128)S(1)}, f32[2,1024,512]{2,1,0:T(8,128)}, u32[]{:S(2)}) copy-start(f32[2,1024,512]{2,1,0:T(8,128)} %get-tuple-element.142) | copy-start | bytes 12582916 | tf_op jit(solution)/shard_map/while
  445.6 6.9 %collective-permute-start = (f32[64,512]{1,0:T(8,128)S(1)}, f32[64,512]{1,0:T(8,128)S(1)}, u32[]{:S(2)}, u32[]{:S(2)}) collective-permute-start(f32[64,512]{1,0:T(8,128)S(1)} %fusion.99), channel_id=1, source_target_pairs={{0,1},{1,2},{2,3},{4,5},{5,6},{6,7},{8,9},{9,10},{10,11},{12,13},{... | collective-permute-start | bytes 393224 | tf_op jit(solution)/shard_map/while/body/eval_jaxpr/ppermute | solution.py:12
  452.5 8.2 %copy-start.2 = (f32[2,1024,64]{2,1,0:T(8,128)S(1)}, f32[2,1024,64]{2,1,0:T(8,128)}, u32[]{:S(2)}) copy-start(f32[2,1024,64]{2,1,0:T(8,128)} %get-tuple-element.143) | copy-start | bytes 1572868 | tf_op jit(solution)/shard_map/while
  455.5 7.1 %copy-start.1 = (f32[2,1024,512]{2,1,0:T(8,128)S(1)}, f32[2,1024,512]{2,1,0:T(8,128)}, u32[]{:S(2)}) copy-start(f32[2,1024,512]{2,1,0:T(8,128)} %get-tuple-element.142) | copy-start | bytes 12582916 | tf_op jit(solution)/shard_map/while
  464.0 6.9 %collective-permute-start = (f32[64,512]{1,0:T(8,128)S(1)}, f32[64,512]{1,0:T(8,128)S(1)}, u32[]{:S(2)}, u32[]{:S(2)}) collective-permute-start(f32[64,512]{1,0:T(8,128)S(1)} %fusion.99), channel_id=1, source_target_pairs={{0,1},{1,2},{2,3},{4,5},{5,6},{6,7},{8,9},{9,10},{10,11},{12,13},{... | collective-permute-start | bytes 393224 | tf_op jit(solution)/shard_map/while/body/eval_jaxpr/ppermute | solution.py:12
  470.9 8.2 %copy-start.2 = (f32[2,1024,64]{2,1,0:T(8,128)S(1)}, f32[2,1024,64]{2,1,0:T(8,128)}, u32[]{:S(2)}) copy-start(f32[2,1024,64]{2,1,0:T(8,128)} %get-tuple-element.143) | copy-start | bytes 1572868 | tf_op jit(solution)/shard_map/while
  473.9 7.1 %copy-start.1 = (f32[2,1024,512]{2,1,0:T(8,128)S(1)}, f32[2,1024,512]{2,1,0:T(8,128)}, u32[]{:S(2)}) copy-start(f32[2,1024,512]{2,1,0:T(8,128)} %get-tuple-element.142) | copy-start | bytes 12582916 | tf_op jit(solution)/shard_map/while
  482.4 6.9 %collective-permute-start = (f32[64,512]{1,0:T(8,128)S(1)}, f32[64,512]{1,0:T(8,128)S(1)}, u32[]{:S(2)}, u32[]{:S(2)}) collective-permute-start(f32[64,512]{1,0:T(8,128)S(1)} %fusion.99), channel_id=1, source_target_pairs={{0,1},{1,2},{2,3},{4,5},{5,6},{6,7},{8,9},{9,10},{10,11},{12,13},{... | collective-permute-start | bytes 393224 | tf_op jit(solution)/shard_map/while/body/eval_jaxpr/ppermute | solution.py:12
  489.6 3.7 copy-start.13
  489.6 5.0 copy-start.3
  493.3 1.2 copy-start.4
Sparse Core Ops, SparseCore 0:
  12.3 186.4 all-reduce.2
  233.2 180.4 all-reduce.4
where the time goes:
time: 516 us; the launch traced here: 515 us
  waiting for transfers between devices  356 us (69%)
  matrix products  82.4 us (16%)
  other arithmetic  32.1 us (6%)
  local copies, waits for them, and re-layouts  19 us (4%)
  between operations  14.4 us (3%)
  starting transfers between devices  10.2 us (2%)
    psum x1, waiting for transfers between devices, shards(): schur_full = lax.psum(schur_terms, 'col')  175 us
    psum x1, waiting for transfers between devices, shards(): sketched = lax.psum(sketch_terms, 'col')  171 us
    dot_general x6, matrix products, last_state(): jnp.einsum('nr,nc->rc', right_wide[position], solved, precision=HIGHEST_P...  20 us
    dot_general x6, matrix products, last_state(): jnp.dot(feed_columns[position], prior_state, precision=HIGHEST_PRECISION)  14.3 us
    another operation x4, other arithmetic, lower_inverse(): gram_lower = jnp.linalg.cholesky(gram_matrix)  12.6 us
    another operation x3, other arithmetic, lower_inverse(): lax.linalg.triangular_solve(gram_lower, identity_matrix, left_side=True,...  11.5 us
    ppermute x3, waiting for transfers between devices, from_behind(): return lax.ppermute(block, axis, route)  10.4 us
  transfers between devices with their start and end apart: 5, of which 5 were waited for; matrix products, arithmetic and copies ran while one was open for 4% of the time, Pallas kernels for 0%

commit v1 on v0

--- a/solution.py
+++ b/solution.py
@@ -62,7 +62,8 @@
     schur_terms = jnp.einsum(
         "jns,jbst->bnt", widened(row_left), middle, precision=HIGHEST_PRECISION
     )
-    schur_full = lax.psum(schur_terms, "col")
+    parts = lax.all_gather(schur_terms, "col", axis=0, tiled=False)
+    schur_full = parts.sum(axis=0)
     slab_rows = schur_full.shape[1] // lax.axis_size("col")
     schur_right = lax.dynamic_slice_in_dim(
         schur_full, lax.axis_index("col") * slab_rows, slab_rows, 1

time: 516 us -> 489 us (0.948)
  waiting for transfers between devices: 356 us -> 318 us
  local copies, waits for them, and re-layouts: 19 us -> 35.8 us
  matrix products: 82.4 us -> 71 us
  other arithmetic: 32.1 us -> 38.5 us
    psum x1 -> x0, waiting for transfers between devices: 175 us -> none  [shards(): schur_full = lax.psum(schur_terms, 'col')]
    all_gather x0 -> x1, waiting for transfers between devices: none -> 121 us  [shards(): parts = lax.all_gather(schur_terms, 'col', axis=0, tiled=False)]
    another operation x0 -> x3, local copies, waits for them, and re-layouts: none -> 16.2 us
    psum x1, waiting for transfers between devices: 171 us -> 186 us  [shards(): sketched = lax.psum(sketch_terms, 'col')]
    reduce_sum x0 -> x1, other arithmetic: none -> 12.9 us  [shards(): schur_full = parts.sum(axis=0)]
    unnamed x32 -> x49, local copies, waits for them, and re-layouts: 7.46 us -> 11.8 us
  transfers between devices with their start and end apart: 5 -> 5, of which waited for: 5 -> 5; matrix products, arithmetic and copies ran while one was open for 4% -> 3% of each run, Pallas kernels for 0% -> 0%
where the time goes in v1:
time: 489 us
  waiting for transfers between devices  318 us (65%)
  matrix products  71 us (15%)
  other arithmetic  38.5 us (8%)
  local copies, waits for them, and re-layouts  35.8 us (7%)
  between operations  14.5 us (3%)
  starting transfers between devices  10.2 us (2%)
    psum x1, waiting for transfers between devices, shards(): sketched = lax.psum(sketch_terms, 'col')  186 us
    all_gather x1, waiting for transfers between devices, shards(): parts = lax.all_gather(schur_terms, 'col', axis=0, tiled=False)  121 us
    dot_general x6, matrix products, last_state(): jnp.einsum('nr,nc->rc', right_wide[position], solved, precision=HIGHEST_P...  16.4 us
    another operation x3, local copies, waits for them, and re-layouts  16.2 us
    dot_general x6, matrix products, last_state(): jnp.dot(feed_columns[position], prior_state, precision=HIGHEST_PRECISION)  14.3 us
    reduce_sum x1, other arithmetic, shards(): schur_full = parts.sum(axis=0)  12.9 us
    another operation x4, other arithmetic, lower_inverse(): gram_lower = jnp.linalg.cholesky(gram_matrix)  11.9 us
    unnamed x49, local copies, waits for them, and re-layouts  11.8 us
  transfers between devices with their start and end apart: 5, of which 5 were waited for; matrix products, arithmetic and copies ran while one was open for 3% of the time, Pallas kernels for 0%

profile of v1, /device:TPU:2, one launch (start us, length us, event | category | flops | bytes accessed | tf_op | source)
XLA Modules:
  0.0 488.6 jit_solution(5633369687149564051)
XLA Ops:
  7.2 1.3 fusion.27
  10.1 2.2 convolution_bitcast_fusion.2
  12.4 186.3 %all-reduce.2.cloned.1.call-done = f32[2,1024,64]{1,2,0:T(8,128)} async-done(((f32[2,1024,64]{1,2,0:T(8,128)}), f32[2,1024,64]{1,2,0:T(8,128)}) %all-reduce.2.cloned.1.call-update) | async-done | bytes 524304 | tf_op jit(solution)/shard_map/psum | solution.py:56
  198.7 1.9 fusion.43
  200.7 11.7 %custom-call.7 = f32[2,64,64]{2,1,0:T(8,128)S(1)} custom-call(f32[2,64,64]{2,1,0:T(8,128)S(1)} %fusion.39), custom_call_target="Cholesky" | custom-call | tf_op jit(solution)/shard_map/jit(cholesky)/cholesky | solution.py:20
  212.6 9.8 %custom-call.8 = f32[2,1,64,64]{2,3,1,0:T(8,128)S(1)} custom-call(f32[2,1,64,64]{3,2,1,0:T(8,128)S(1)} %select_bitcast_fusion), custom_call_target="InvertDiagBlocksLowerTriangular" | custom-call | tf_op jit(solution)/shard_map/triangular_solve | solution.py:24
  226.0 4.0 copy.42
  230.0 3.6 fusion.49
  233.7 1.3 copy.46
  237.2 2.5 convolution_convert_fusion
  239.7 1.3 fusion.46
  241.0 1.3 copy-done.4
  242.3 2.0 fusion.47
  244.3 120.7 %all-gather.3.cloned.1.call-done = f32[128,1024,64]{1,2,0:T(8,128)} async-done(((f32[2,1024,64]{1,2,0:T(8,128)}), f32[128,1024,64]{1,2,0:T(8,128)}) %all-gather.3.cloned.1.call-update) | async-done | bytes 33554448 | tf_op jit(solution)/shard_map/all_gather | solution.py:65
  364.9 12.9 %reduce_sum.9 = f32[2,1024,64]{1,2,0:T(8,128)} reduce(f32[64,2,1024,64]{2,3,1,0:T(8,128)} %bitcast.172, f32[]{:T(128)} %constant.54.clone.1), dimensions={0}, to_apply=%region_3.4 | reduce | flops 8257536 | bytes 34078724 | tf_op jit(solution)/shard_map/reduce_sum | solution.py:66
  377.8 3.3 fusion.23
  381.2 3.5 fusion.48
  384.8 2.2 fusion.20
  387.0 4.3 convolution_bitcast_fusion
  391.4 5.4 %copy.45 = f32[2,1024,512]{2,1,0:T(8,128)} copy(f32[2,1024,512]{1,2,0:T(8,128)} %convolution_bitcast_fusion) | data formatting | bytes 8388608 | tf_op jit(solution)/shard_map/while | solution.py:103
  396.8 68.7 %while.10 = (s32[]{:T(128)}, f32[64,512]{1,0:T(8,128)S(1)}, pred[]{:T(512)}, f32[2,1024,512]{2,1,0:T(8,128)}, f32[2,1024,64]{2,1,0:T(8,128)}, /*index=5*/f32[2,1...) while((s32[]{:T(128)}, f32[64,512]{1,0:T(8,128)S(1)}, pred[]{:T(512)}, f32[2,1024,512]{2,1,0:T(8,128)}, ...), condition=%wide.region_5.6_spmd, body=%wide.region_4.5_spmd.sunk | while | flops 1611694080 | bytes 43385012 | solution.py:103
  396.8 5.4 %copy.60 = f32[2,1024,512]{1,2,0:T(8,128)} copy(f32[2,1024,512]{2,1,0:T(8,128)} %get-tuple-element.153) | data formatting | bytes 8388608 | tf_op jit(solution)/shard_map
  402.2 2.9 fusion.101
  405.1 3.2 fusion.102
  408.4 1.9 fusion.103
  410.2 2.2 fusion.104
  412.5 3.4 collective-permute-start
  415.9 4.2 collective-permute-done
  420.1 5.4 %copy.60 = f32[2,1024,512]{1,2,0:T(8,128)} copy(f32[2,1024,512]{2,1,0:T(8,128)} %get-tuple-element.153) | data formatting | bytes 8388608 | tf_op jit(solution)/shard_map
  425.5 2.9 fusion.101
  428.4 3.2 fusion.102
  431.6 1.9 fusion.103
  433.5 2.2 fusion.104
  435.8 3.4 collective-permute-start
  439.1 3.5 collective-permute-done
  442.7 5.4 %copy.60 = f32[2,1024,512]{1,2,0:T(8,128)} copy(f32[2,1024,512]{2,1,0:T(8,128)} %get-tuple-element.153) | data formatting | bytes 8388608 | tf_op jit(solution)/shard_map
  448.1 2.9 fusion.101
  451.0 3.2 fusion.102
  454.3 1.9 fusion.103
  456.1 2.2 fusion.104
  458.4 3.4 collective-permute-start
  461.8 3.5 collective-permute-done
  465.5 3.7 fusion.22
  469.2 1.2 fusion.30
  470.4 1.9 fusion.21
  472.3 1.2 convolution_bitcast_fusion.3
  473.9 1.5 pad_maximum_fusion
  475.5 3.9 copy.50
  (84 shorter events, 10.4 us)
Async XLA Ops:
  7.2 230.0 %copy-start = (bf16[1024,1024]{1,0:T(8,128)(2,1)S(1)}, bf16[1024,1024]{1,0:T(8,128)(2,1)}, u32[]{:S(2)}) copy-start(bf16[1024,1024]{1,0:T(8,128)(2,1)} %param.23) | copy-start | bytes 6291460
  7.2 191.5 %all-reduce.2.cloned.1.call-start = ((), (), s32[]{:S(2)}) async-start(), calls=%async_computation | async-start | bytes 1048576 | tf_op jit(solution)/shard_map/psum | solution.py:56
  10.1 214.1 %copy-start.19 = (bf16[1,2,1024,64]{2,3,1,0:T(8,128)(2,1)S(1)}, bf16[1,2,1024,64]{2,3,1,0:T(8,128)(2,1)}, u32[]{:S(2)}) copy-start(bf16[1,2,1024,64]{2,3,1,0:T(8,128)(2,1)} %param.16) | copy-start | bytes 786436
  12.2 212.5 %copy-start.20 = (bf16[1,1024,64]{1,2,0:T(8,128)(2,1)S(1)}, bf16[1,1024,64]{1,2,0:T(8,128)(2,1)}, u32[]{:S(2)}) copy-start(bf16[1,1024,64]{1,2,0:T(8,128)(2,1)} %param.18) | copy-start | bytes 393220
  12.3 352.7 %all-gather.3.cloned.1.call-start = ((), (), s32[]{:S(2)}) async-start(), calls=%async_computation.1 | async-start | bytes 34078720 | tf_op jit(solution)/shard_map/all_gather | solution.py:65
  198.7 24.1 %copy-start.13 = (f32[2,1024,64]{1,2,0:T(8,128)S(1)}, f32[2,1024,64]{1,2,0:T(8,128)}, u32[]{:S(2)}) copy-start(f32[2,1024,64]{1,2,0:T(8,128)} %all-reduce.2.cloned.1.call-done) | copy-start | bytes 1572868
  223.4 0.8 copy-start.10
  226.0 4.0 copy-start.21
  230.0 5.0 %copy-start.16 = (bf16[2,1024,64]{1,2,0:T(8,128)(2,1)S(1)}, bf16[2,1024,64]{1,2,0:T(8,128)(2,1)}, u32[]{:S(2)}) copy-start(bf16[2,1024,64]{1,2,0:T(8,128)(2,1)} %param.26) | copy-start | bytes 786436
  233.6 1.3 copy-start.8
  233.6 3.5 copy-start.12
  239.6 1.3 copy-start.15
  239.7 2.6 copy-start.22
  240.9 1.3 copy-start.4
  364.9 12.9 %copy-start.5 = (f32[512,1024]{1,0:T(8,128)S(1)}, f32[512,1024]{1,0:T(8,128)}, u32[]{:S(2)}) copy-start(f32[512,1024]{1,0:T(8,128)} %copy-done.4) | copy-start | bytes 6291460
  377.8 3.4 copy-start.11
  381.2 3.6 copy-start.7
  381.2 3.6 copy-start.18
  381.2 3.6 copy-start.23
  384.8 2.3 copy-start.14
  402.2 6.2 %copy-start.3 = (f32[2,1024,64]{2,1,0:T(8,128)S(1)}, f32[2,1024,64]{2,1,0:T(8,128)}, u32[]{:S(2)}) copy-start(f32[2,1024,64]{2,1,0:T(8,128)} %get-tuple-element.154) | copy-start | bytes 1572868 | tf_op jit(solution)/shard_map/while
  405.1 5.1 %copy-start.2 = (f32[2,1024,512]{1,2,0:T(8,128)S(1)}, f32[2,1024,512]{1,2,0:T(8,128)}, u32[]{:S(2)}) copy-start(f32[2,1024,512]{1,2,0:T(8,128)} %copy.60) | copy-start | bytes 12582916 | tf_op jit(solution)/shard_map/while
  412.5 7.5 %collective-permute-start = (f32[64,512]{1,0:T(8,128)S(1)}, f32[64,512]{1,0:T(8,128)S(1)}, u32[]{:S(2)}, u32[]{:S(2)}) collective-permute-start(f32[64,512]{1,0:T(8,128)S(1)} %fusion.104), channel_id=1, source_target_pairs={{0,1},{1,2},{2,3},{4,5},{5,6},{6,7},{8,9},{9,10},{10,11},{12,13},{... | collective-permute-start | bytes 393224 | tf_op jit(solution)/shard_map/while/body/eval_jaxpr/ppermute | solution.py:12
  425.5 6.2 %copy-start.3 = (f32[2,1024,64]{2,1,0:T(8,128)S(1)}, f32[2,1024,64]{2,1,0:T(8,128)}, u32[]{:S(2)}) copy-start(f32[2,1024,64]{2,1,0:T(8,128)} %get-tuple-element.154) | copy-start | bytes 1572868 | tf_op jit(solution)/shard_map/while
  428.4 5.1 %copy-start.2 = (f32[2,1024,512]{1,2,0:T(8,128)S(1)}, f32[2,1024,512]{1,2,0:T(8,128)}, u32[]{:S(2)}) copy-start(f32[2,1024,512]{1,2,0:T(8,128)} %copy.60) | copy-start | bytes 12582916 | tf_op jit(solution)/shard_map/while
  435.8 6.9 %collective-permute-start = (f32[64,512]{1,0:T(8,128)S(1)}, f32[64,512]{1,0:T(8,128)S(1)}, u32[]{:S(2)}, u32[]{:S(2)}) collective-permute-start(f32[64,512]{1,0:T(8,128)S(1)} %fusion.104), channel_id=1, source_target_pairs={{0,1},{1,2},{2,3},{4,5},{5,6},{6,7},{8,9},{9,10},{10,11},{12,13},{... | collective-permute-start | bytes 393224 | tf_op jit(solution)/shard_map/while/body/eval_jaxpr/ppermute | solution.py:12
  448.1 6.2 %copy-start.3 = (f32[2,1024,64]{2,1,0:T(8,128)S(1)}, f32[2,1024,64]{2,1,0:T(8,128)}, u32[]{:S(2)}) copy-start(f32[2,1024,64]{2,1,0:T(8,128)} %get-tuple-element.154) | copy-start | bytes 1572868 | tf_op jit(solution)/shard_map/while
  451.0 5.1 %copy-start.2 = (f32[2,1024,512]{1,2,0:T(8,128)S(1)}, f32[2,1024,512]{1,2,0:T(8,128)}, u32[]{:S(2)}) copy-start(f32[2,1024,512]{1,2,0:T(8,128)} %copy.60) | copy-start | bytes 12582916 | tf_op jit(solution)/shard_map/while
  458.4 6.9 %collective-permute-start = (f32[64,512]{1,0:T(8,128)S(1)}, f32[64,512]{1,0:T(8,128)S(1)}, u32[]{:S(2)}, u32[]{:S(2)}) collective-permute-start(f32[64,512]{1,0:T(8,128)S(1)} %fusion.104), channel_id=1, source_target_pairs={{0,1},{1,2},{2,3},{4,5},{5,6},{6,7},{8,9},{9,10},{10,11},{12,13},{... | collective-permute-start | bytes 393224 | tf_op jit(solution)/shard_map/while/body/eval_jaxpr/ppermute | solution.py:12
  465.5 3.7 copy-start.17
  465.5 4.9 %copy-start.6 = (f32[2,1024,512]{1,2,0:T(8,128)S(1)}, f32[2,1024,512]{1,2,0:T(8,128)}, u32[]{:S(2)}) copy-start(f32[2,1024,512]{1,2,0:T(8,128)} %convolution_bitcast_fusion) | copy-start | bytes 12582916
  469.2 1.2 copy-start.9
  473.9 7.8 %copy-start.1 = (bf16[1024,1024]{1,0:T(8,128)(2,1)S(1)}, bf16[1024,1024]{1,0:T(8,128)(2,1)}, u32[]{:S(2)}) copy-start(bf16[1024,1024]{1,0:T(8,128)(2,1)} %param.23) | copy-start | bytes 6291460
Sparse Core Ops, SparseCore 0:
  12.4 186.2 all-reduce.1
  226.1 138.7 all-gather.2
